TPU v7x, 32 devices: a whole 2x2x4 slice. The times are simulated.
32 devices in a mesh: clips: 2 (over y), tm: 4 (over x, core), rows: 4 (over z).
Axes of the slice: x: 2, y: 2, z: 4, core: 2. Of those that a mesh axis runs over, the one named last changes fastest.
Arguments:
- features: bfloat16 [64, 16, 32, 192], P(('clips', 'tm'), 'rows'), parts along dimension 0, may hold values from -6 to 6
- norm_gain: float32 [192], replicated, may hold values from 0.1 to 1.9
- conv_weight: bfloat16 [3, 3, 3, 192, 96], replicated, may hold values from -0.078125 to 0.078125
- out_grad: bfloat16 [64, 16, 32, 96], P(('clips', 'tm'), 'rows'), parts along dimension 0, may hold values from -6 to 6
Outputs:
- grad_features: bfloat16 [64, 16, 32, 192], P(('clips', 'tm'), 'rows'), parts along dimension 0
- grad_weight: float32 [6, 3, 3, 192, 96], P('clips'), parts along dimension 0
There are 2 independent parts, one for each index of `clips`. A program takes and returns all parts, laid end to end along the dimension named above; an argument that names none is the same for every part. Nothing has to cross between parts.
All inputs are finite; a program needn't handle non-finite values.
Results may differ from a plain program's by a relative error of at most 0.0029.
Values may be sent and summed in bfloat16 or wider, within the bound.
A program may use at most 64 MiB of HBM per device.

v0:
```python
import jax
import jax.numpy as jnp
from jax import lax
from jax.sharding import PartitionSpec as P


def passed_along(block, axis, distance):
    devices = range(lax.axis_size(axis))
    route = [(i - distance, i) for i in devices if i - distance in devices]
    return lax.ppermute(block, axis, route)


def with_halo(cells, sides, width):
    for axis, dim in sides:
        count = lax.axis_size(axis)
        ends = count - 1
        head = lax.slice_in_dim(cells, 0, width, axis=dim)
        tail = lax.slice_in_dim(cells, cells.shape[dim] - width, cells.shape[dim], axis=dim)
        cells = jnp.concatenate(
            [
                lax.ppermute(tail, axis, [(i, (i + 1) % count) for i in range(ends)]),
                cells,
                lax.ppermute(head, axis, [((i + 1) % count, i) for i in range(ends)]),
            ],
            axis=dim,
        )
    return cells


def activate(features, norm_gain):
    values = features.astype(jnp.float32)
    inv_rms = lax.rsqrt(jnp.mean(values * values, axis=-1, keepdims=True) + 1e-06)
    unit = values * inv_rms
    normed = unit * norm_gain
    return (normed, inv_rms, unit)


def pad_columns(block):
    return jnp.pad(block, ((0, 0), (0, 0), (1, 1), (0, 0)))


def on_device(features, norm_gain, conv_weight, out_grad):
    frames, height, width, channels = features.shape
    outputs = out_grad.shape[3]
    normed, inv_rms, unit = activate(features, norm_gain)
    before = passed_along(features[frames - 2 :], "tm", 1)
    extended = jnp.concatenate([before, features], axis=0)
    framed = with_halo(extended, (("rows", 1),), 1)
    rim_normed = activate(framed, norm_gain)[0]
    act_pad = pad_columns(jax.nn.silu(rim_normed).astype(jnp.bfloat16))
    after = passed_along(out_grad[:2], "tm", -1)
    later = jnp.concatenate([out_grad, after], axis=0)
    out_pad = pad_columns(with_halo(later, (("rows", 1),), 1))
    count = frames * height * width
    flat_out = out_grad.reshape(count, outputs)
    grad_act = jnp.zeros((count, channels), jnp.float32)
    kernel_terms = []
    for i in range(3):
        for j in range(3):
            for k in range(3):
                shifted = out_pad[
                    2 - i : 2 - i + frames, 2 - j : 2 - j + height, 2 - k : 2 - k + width
                ].reshape(count, outputs)
                grad_act = grad_act + jnp.dot(
                    shifted, conv_weight[i, j, k].T, preferred_element_type=jnp.float32
                )
                window = act_pad[i : i + frames, j : j + height, k : k + width].reshape(
                    count, channels
                )
                kernel_terms.append(jnp.dot(window.T, flat_out, preferred_element_type=jnp.float32))
    positions = count * lax.axis_size("tm") * lax.axis_size("rows")
    scale = 1.0 / jnp.sqrt(jnp.float32(positions))
    kernel_local = jnp.stack(kernel_terms).reshape(27 * channels, outputs) * scale
    kernel_total = lax.psum(kernel_local, ("tm", "rows"))
    grad_weight = kernel_total.reshape(3, 3, 3, channels, outputs)
    grad_act = grad_act.reshape(frames, height, width, channels)
    sigma = jax.nn.sigmoid(normed)
    grad_normed = grad_act * sigma * (1.0 + normed * (1.0 - sigma))
    grad_unit = grad_normed * norm_gain
    grad_features = inv_rms * (
        grad_unit - unit * jnp.mean(grad_unit * unit, axis=-1, keepdims=True)
    )
    return (grad_features.astype(jnp.bfloat16), grad_weight)


def solution(mesh):
    placed = (
        P(("clips", "tm"), "rows", None, None),
        P(),
        P(),
        P(("clips", "tm"), "rows", None, None),
    )
    return jax.shard_map(
        on_device,
        mesh=mesh,
        in_specs=placed,
        out_specs=(P(("clips", "tm"), "rows", None, None), P("clips", None, None, None, None)),
        check_vma=False,
    )
```

profile of v0, /device:TPU:0, one launch (start us, length us, event | category | flops | bytes accessed | tf_op | source)
XLA Modules:
  0.0 162.6 jit_solution(9131415052138803827)
XLA Ops:
  7.2 0.9 slice.286
  8.1 1.3 collective-permute-start
  9.4 0.9 slice.342
  10.3 3.0 %collective-permute-start.3 = (bf16[2,4,32,192]{3,2,1,0:T(8,128)(2,1)S(1)}, bf16[2,4,32,192]{3,2,1,0:T(8,128)(2,1)S(1)}, u32[]{:S(2)}, u32[]{:S(2)}) collective-permute-start(bf16[2,4,32,192]{3,2,1,0:T(8,128)(2,1)S(1)} %slice.342), channel_id=1, source_target_pairs={{0,4},{4,8},{8,12},{1,5},{5,9},{9,13},{2,6},{6,10},{10,14},{3,7},{... | collective-permute-start | bytes 294920 | tf_op jit(solution)/shard_map/ppermute | solution.py:10
  13.4 1.3 fusion.55
  14.7 1.0 constant_dynamic-update-slice_fusion.1
  15.7 1.3 collective-permute-start.2
  17.0 5.6 %collective-permute-start.1 = (bf16[10,1,32,96]{3,2,1,0:T(8,128)(2,1)S(1)}, bf16[10,1,32,96]{3,2,1,0:T(8,128)(2,1)S(1)}, u32[]{:S(2)}, u32[]{:S(2)}) collective-permute-start(bf16[10,1,32,96]{3,2,1,0:T(8,128)(2,1)S(1)} %get-tuple-element.33), channel_id=1, source_target_pairs={{0,1},{1,2},{2,3},{4,5},{5,6},{6,7},{8,9},{9,10},{10,11},{12,13},{... | collective-permute-start | bytes 184328 | tf_op jit(solution)/shard_map/ppermute | solution.py:21
  22.7 1.3 collective-permute-start.5
  24.0 4.6 %collective-permute-start.4 = (bf16[10,1,32,192]{3,2,1,0:T(8,128)(2,1)S(1)}, bf16[10,1,32,192]{3,2,1,0:T(8,128)(2,1)S(1)}, u32[]{:S(2)}, u32[]{:S(2)}) collective-permute-start(bf16[10,1,32,192]{3,2,1,0:T(8,128)(2,1)S(1)} %get-tuple-element.2), channel_id=1, source_target_pairs={{0,1},{1,2},{2,3},{4,5},{5,6},{6,7},{8,9},{9,10},{10,11},{12,13},{... | collective-permute-start | bytes 368648 | tf_op jit(solution)/shard_map/ppermute | solution.py:21
  28.8 0.9 fusion.143
  29.8 0.4 copy-done.2
  31.2 0.9 pad_maximum_fusion.1
  37.0 0.4 copy-done.1
  38.5 0.3 fusion
  38.9 0.7 fusion.7
  46.4 0.5 fusion.30
  48.6 1.7 %broadcast_multiply_fusion = f32[27,192,96]{2,1,0:T(8,128)} fusion(f32[27,192,96]{2,1,0:T(8,128)S(1)} %fusion.27), kind=kLoop, calls=%fused_computation.12 | loop fusion | flops 497664 | bytes 3981312 | tf_op jit(solution)/shard_map/mul | solution.py:73
  50.3 0.9 copy-done.3
  51.2 1.1 fusion.11
  52.7 1.4 fusion.51
  54.1 1.4 fusion.54
  55.5 96.7 %all-reduce.4.cloned.1.call-done = f32[3,3,3,192,96]{4,3,2,1,0:T(8,128)} async-done(((f32[3,3,3,192,96]{4,3,2,1,0:T(8,128)}), f32[3,3,3,192,96]{4,3,2,1,0:T(8,128)}) %all-reduce.4.cloned.1.call-update) | async-done | bytes 1990672 | tf_op jit(solution)/shard_map/psum | solution.py:74
  152.3 3.5 %copy.64 = f32[3,3,3,192,96]{4,3,2,1,0:T(8,128)} copy(f32[3,3,3,192,96]{4,3,2,1,0:T(8,128)} %all-reduce.4.cloned.1.call-done) | data formatting | bytes 3981312
  (79 shorter events, 16.0 us)
Async XLA Ops:
  7.2 15.4 %copy-start = (bf16[8,4,32,192]{3,2,1,0:T(8,128)(2,1)S(1)}, bf16[8,4,32,192]{3,2,1,0:T(8,128)(2,1)}, u32[]{:S(2)}) copy-start(bf16[8,4,32,192]{3,2,1,0:T(8,128)(2,1)} %param.4) | copy-start | bytes 1179652
  7.2 145.1 %all-reduce.4.cloned.1.call-start = ((), (), s32[]{:S(2)}) async-start(), calls=%async_computation | async-start | bytes 5308416 | tf_op jit(solution)/shard_map/psum | solution.py:74
  8.1 7.5 %collective-permute-start = (bf16[2,4,32,96]{3,2,1,0:T(8,128)(2,1)S(1)}, bf16[2,4,32,96]{3,2,1,0:T(8,128)(2,1)S(1)}, u32[]{:S(2)}, u32[]{:S(2)}) collective-permute-start(bf16[2,4,32,96]{3,2,1,0:T(8,128)(2,1)S(1)} %slice.286), channel_id=1, source_target_pairs={{4,0},{8,4},{12,8},{5,1},{9,5},{13,9},{6,2},{10,6},{14,10},{7,3},{... | collective-permute-start | bytes 147464 | tf_op jit(solution)/shard_map/ppermute | solution.py:10
  10.3 12.3 %collective-permute-start.3 = (bf16[2,4,32,192]{3,2,1,0:T(8,128)(2,1)S(1)}, bf16[2,4,32,192]{3,2,1,0:T(8,128)(2,1)S(1)}, u32[]{:S(2)}, u32[]{:S(2)}) collective-permute-start(bf16[2,4,32,192]{3,2,1,0:T(8,128)(2,1)S(1)} %slice.342), channel_id=1, source_target_pairs={{0,4},{4,8},{8,12},{1,5},{5,9},{9,13},{2,6},{6,10},{10,14},{3,7},{... | collective-permute-start | bytes 294920 | tf_op jit(solution)/shard_map/ppermute | solution.py:10
  15.7 12.9 %collective-permute-start.2 = (bf16[10,1,32,96]{3,2,1,0:T(8,128)(2,1)S(1)}, bf16[10,1,32,96]{3,2,1,0:T(8,128)(2,1)S(1)}, u32[]{:S(2)}, u32[]{:S(2)}) collective-permute-start(bf16[10,1,32,96]{3,2,1,0:T(8,128)(2,1)S(1)} %get-tuple-element.34), channel_id=1, source_target_pairs={{1,0},{2,1},{3,2},{5,4},{6,5},{7,6},{9,8},{10,9},{11,10},{13,12},{... | collective-permute-start | bytes 184328 | tf_op jit(solution)/shard_map/ppermute | solution.py:23
  17.0 11.6 %collective-permute-start.1 = (bf16[10,1,32,96]{3,2,1,0:T(8,128)(2,1)S(1)}, bf16[10,1,32,96]{3,2,1,0:T(8,128)(2,1)S(1)}, u32[]{:S(2)}, u32[]{:S(2)}) collective-permute-start(bf16[10,1,32,96]{3,2,1,0:T(8,128)(2,1)S(1)} %get-tuple-element.33), channel_id=1, source_target_pairs={{0,1},{1,2},{2,3},{4,5},{5,6},{6,7},{8,9},{9,10},{10,11},{12,13},{... | collective-permute-start | bytes 184328 | tf_op jit(solution)/shard_map/ppermute | solution.py:21
  22.7 15.8 %collective-permute-start.5 = (bf16[10,1,32,192]{3,2,1,0:T(8,128)(2,1)S(1)}, bf16[10,1,32,192]{3,2,1,0:T(8,128)(2,1)S(1)}, u32[]{:S(2)}, u32[]{:S(2)}) collective-permute-start(bf16[10,1,32,192]{3,2,1,0:T(8,128)(2,1)S(1)} %get-tuple-element.3), channel_id=1, source_target_pairs={{1,0},{2,1},{3,2},{5,4},{6,5},{7,6},{9,8},{10,9},{11,10},{13,12},{... | collective-permute-start | bytes 368648 | tf_op jit(solution)/shard_map/ppermute | solution.py:23
  24.0 14.5 %collective-permute-start.4 = (bf16[10,1,32,192]{3,2,1,0:T(8,128)(2,1)S(1)}, bf16[10,1,32,192]{3,2,1,0:T(8,128)(2,1)S(1)}, u32[]{:S(2)}, u32[]{:S(2)}) collective-permute-start(bf16[10,1,32,192]{3,2,1,0:T(8,128)(2,1)S(1)} %get-tuple-element.2), channel_id=1, source_target_pairs={{0,1},{1,2},{2,3},{4,5},{5,6},{6,7},{8,9},{9,10},{10,11},{12,13},{... | collective-permute-start | bytes 368648 | tf_op jit(solution)/shard_map/ppermute | solution.py:21
  28.8 1.3 copy-start.2
  36.5 1.0 copy-start.1
  38.0 0.9 copy-start.4
  50.3 0.9 copy-start.3
  52.3 1.8 %copy-start.5 = (f32[192]{0:T(256)S(1)}, f32[192]{0:T(256)}, u32[]{:S(2)}) copy-start(f32[192]{0:T(256)} %param.5) | copy-start | bytes 2308
Sparse Core Ops, SparseCore 0:
  50.4 101.7 all-reduce.3
where the time goes:
time: 163 us
  waiting for transfers between devices  96.8 us (59%)
  starting transfers between devices  17.1 us (10%)
  matrix products  16.7 us (10%)
  between operations  14.7 us (9%)
  local copies, waits for them, and re-layouts  9.4 us (6%)
  other arithmetic  7.98 us (5%)
    psum x1, waiting for transfers between devices, on_device(): kernel_total = lax.psum(kernel_local, ('tm', 'rows'))  96.7 us
    ppermute x2, starting transfers between devices, with_halo(): lax.ppermute(tail, axis, [(i, (i + 1) % count) for i in range(ends)])  10.1 us
    dot_general x27, matrix products, on_device(): jnp.dot(window.T, flat_out, preferred_element_type=jnp.float32)  8.8 us
    dot_general x27, matrix products, on_device(): jnp.dot(shifted, conv_weight[i, j, k].T, preferred_element_type=jnp.float32)  7.93 us
    unnamed x15, local copies, waits for them, and re-layouts  6.21 us
    ppermute x2, starting transfers between devices, passed_along(): return lax.ppermute(block, axis, route)  4.32 us
  transfers between devices with their start and end apart: 7, of which 1 were waited for; matrix products, arithmetic and copies ran while one was open for 10% of the time, Pallas kernels for 0%

commit v1 on v0

v1 whole, which is shorter than its diff:
```python
import functools
import math

import jax
import jax.numpy as jnp
from jax import lax
from jax.experimental import pallas as pl
from jax.experimental.pallas import tpu as pltpu
from jax.sharding import PartitionSpec as P

LANES = 128
SUB = 16
MESH = pl.DeviceIdType.MESH
NT = (((1,), (1,)), ((), ()))


def shift_lanes(x, shift):
    shift = shift % LANES
    return x if shift == 0 else pltpu.roll(x, shift, 1)


def rearrange(sources, source_width, target_start, target_width):
    lane = lax.broadcasted_iota(jnp.int32, (1, LANES), 1)
    value = None
    for a, source in enumerate(sources):
        first = a * source_width - target_start
        if first >= target_width or first + source_width <= 0:
            continue
        moved = shift_lanes(source, first)
        value = moved if value is None else jnp.where(lane >= first, moved, value)
    return value


def kernel(
    dims,
    features, gain, weight, grad,
    gf_ref, out_ref,
    padded, shifted, wide, act_t, acc, parts, gwf, send_a, recv_a, sum_a,
    send_b, recv_b, sum_b, send_c, recv_c, gath,
    halo_s, halo_r, sa, ra, sb, rb, sc, rc, sc2, rc2, sb2, rb2, sa2, ra2, out_sem,
):
    T, R, PR, X, m = dims
    frames, height, width, channels = features.shape
    outputs = grad.shape[3]
    taps = weight.shape[0]
    tm, z = lax.axis_index("tm"), lax.axis_index("rows")
    pair, x = lax.rem(tm, PR), lax.div(tm, PR)

    barrier = pltpu.get_barrier_semaphore()
    for d in range(1, T * R):
        peer = lax.rem(tm * R + z + d, T * R)
        pl.semaphore_signal(
            barrier, inc=1, device_id={"tm": lax.div(peer, R), "rows": lax.rem(peer, R)},
            device_id_type=MESH,
        )

    up, down, later, earlier = z > 0, z < R - 1, tm < T - 1, tm > 0
    own = pl.ds(1, height)
    tail = pl.ds(frames, 2)
    body = pl.ds(0, frames)
    halos = (
        (down, (tm, z + 1), up, grad.at[:, height - 1], padded.at[body, 0]),
        (up, (tm, z - 1), down, grad.at[:, 0], padded.at[body, height + 1]),
        (earlier, (tm - 1, z), later, grad.at[pl.ds(0, 2)], padded.at[tail, own]),
        (jnp.logical_and(earlier, down), (tm - 1, z + 1), jnp.logical_and(later, up),
         grad.at[pl.ds(0, 2), height - 1], padded.at[tail, 0]),
        (jnp.logical_and(earlier, up), (tm - 1, z - 1), jnp.logical_and(later, down),
         grad.at[pl.ds(0, 2), 0], padded.at[tail, height + 1]),
    )

    def halo(n):
        _, to, _, source, target = halos[n]
        return pltpu.make_async_remote_copy(
            src_ref=source, dst_ref=target, send_sem=halo_s.at[n], recv_sem=halo_r.at[n],
            device_id={"tm": to[0], "rows": to[1]}, device_id_type=MESH,
        )

    for n, (_, _, receives, _, target) in enumerate(halos):
        @pl.when(jnp.logical_not(receives))
        def _():
            target[...] = jnp.zeros(target.shape, target.dtype)

    pl.semaphore_wait(barrier, T * R - 1)
    for n in range(5):
        @pl.when(halos[n][0])
        def _():
            halo(n).start()

    def activate(f):
        values = features[f].reshape(height * width, channels).astype(jnp.float32)
        inv_rms = lax.rsqrt(jnp.sum(values * values, axis=-1, keepdims=True) / channels + 1e-06)
        unit = values * inv_rms
        normed = unit * gain[...]
        sigma = 1.0 / (1.0 + jnp.exp(-normed))
        return inv_rms, unit, normed, sigma

    for f in range(frames):
        _, _, normed, sigma = activate(f)
        act = (normed * sigma).astype(jnp.bfloat16)
        act_t[:, f * height * width:(f + 1) * height * width] = act.T
        padded[f, 1:1 + height] = grad[f]

    wide[...] = jnp.zeros(wide.shape, wide.dtype)
    for t in range(taps):
        wide[:, t * LANES:t * LANES + outputs] = weight[t]
    shifted[...] = jnp.zeros(shifted.shape, shifted.dtype)

    for n in range(5):
        @pl.when(halos[n][2])
        def _():
            halo(n).wait_recv()

    rows = (height + 2) * width
    column = lax.rem(lax.broadcasted_iota(jnp.int32, (rows, LANES), 0), width)
    for f in range(frames + 2):
        shifted[f, :, :, LANES:LANES + outputs] = padded[f]
        middle = shifted[f, :, :, LANES:2 * LANES].reshape(rows, LANES).astype(jnp.float32)
        after = jnp.where(column == width - 1, 0.0, pltpu.roll(middle, rows - 1, 0))
        before = jnp.where(column == 0, 0.0, pltpu.roll(middle, 1, 0))
        shape = (height + 2, width, LANES)
        shifted[f, :, :, 0:LANES] = after.astype(jnp.bfloat16).reshape(shape)
        shifted[f, :, :, 2 * LANES:3 * LANES] = before.astype(jnp.bfloat16).reshape(shape)

    count = frames * height * width

    def window(i):
        return jnp.concatenate(
            [
                shifted[2 - i:2 - i + frames, 2 - j:2 - j + height].reshape(count, 3 * LANES)
                for j in range(3)
            ],
            axis=1,
        )

    for i in range(3):
        terms = jnp.dot(act_t[...], window(i), preferred_element_type=jnp.float32)
        for t in range(9):
            parts[9 * i + t] = terms[:, t * LANES:(t + 1) * LANES]

    group = LANES // math.gcd(LANES, outputs)
    per_group = group * outputs // LANES
    row_tiles = channels // SUB
    total = T * R * m
    stored = 0

    def place(n):
        n, s = divmod(n, m)
        n, xx = divmod(n, X)
        pp, c = divmod(n, R)
        return pp, c, xx, s

    for g in range(-(-taps // group)):
        sources = [parts[t] for t in range(g * group, min(taps, (g + 1) * group))]
        for lt in range(per_group):
            tile = rearrange(sources, outputs, lt * LANES, LANES)
            for rt in range(row_tiles):
                where = place(stored)
                piece = tile[rt * SUB:(rt + 1) * SUB]
                gwf[where] = piece
                send_a[where] = piece.astype(jnp.bfloat16)
                stored += 1
    while stored < total:
        gwf[place(stored)] = jnp.zeros((SUB, LANES), jnp.float32)
        send_a[place(stored)] = jnp.zeros((SUB, LANES), jnp.bfloat16)
        stored += 1

    def remote(source, target, send, recv, to_tm, to_z):
        return pltpu.make_async_remote_copy(
            src_ref=source, dst_ref=target, send_sem=send, recv_sem=recv,
            device_id={"tm": to_tm, "rows": to_z}, device_id_type=MESH,
        )

    mate = x * PR + (1 - pair if PR == 2 else pair)

    def chunk(d):
        return lax.rem(z + d, R)

    def stage_a(d):
        c = chunk(d)
        return remote(send_a.at[1 - pair, c], recv_a.at[d - 1], sa.at[d - 1], ra.at[d - 1], mate, z)

    def side(e):
        return lax.rem(x + e, X)

    def stage_b(d, e):
        return remote(
            send_b.at[d - 1, side(e)], recv_b.at[d - 1, e - 1],
            sb.at[d - 1, e - 1], rb.at[d - 1, e - 1], side(e) * PR + pair, z,
        )

    def stage_c(d):
        return remote(send_c.at[d - 1], recv_c.at[d - 1], sc.at[d - 1], rc.at[d - 1], tm, chunk(d))

    def gather_c(d):
        piece = gath.at[pair, z, x]
        return remote(piece, piece, sc2.at[d - 1], rc2.at[d - 1], tm, chunk(d))

    def gather_b(d, e):
        piece = gath.at[pair, lax.rem(z + R - d + R, R), x]
        return remote(piece, piece, sb2.at[d - 1, e - 1], rb2.at[d - 1, e - 1], side(e) * PR + pair, z)

    def gather_a(d):
        piece = gath.at[pair, lax.rem(z + R - d + R, R)]
        return remote(piece, piece, sa2.at[d - 1], ra2.at[d - 1], mate, z)

    order = range(1, R + 1)
    if PR == 2:
        for d in order:
            stage_a(d).start()

    def conv(i):
        weights = wide[:, 9 * LANES * i:9 * LANES * (i + 1)]
        return lax.dot_general(window(i), weights, NT, preferred_element_type=jnp.float32)

    acc[...] = conv(0)

    for d in order:
        value = gwf[pair, chunk(d)]
        if PR == 2:
            stage_a(d).wait_recv()
            value = value + recv_a[d - 1].astype(jnp.float32)
        sum_a[d - 1] = value
        send_b[d - 1] = value.astype(jnp.bfloat16)
        for e in range(1, X):
            stage_b(d, e).start()

    acc[...] += conv(1)

    for d in order:
        value = sum_a[d - 1, x]
        for e in range(1, X):
            stage_b(d, e).wait_recv()
            value = value + recv_b[d - 1, e - 1].astype(jnp.float32)
        if d < R:
            send_c[d - 1] = value.astype(jnp.bfloat16)
            stage_c(d).start()
        else:
            sum_b[...] = value

    acc[...] += conv(2)

    value = sum_b[...]
    for d in range(1, R):
        stage_c(d).wait_recv()
        value = value + recv_c[d - 1].astype(jnp.float32)
    gath[pair, z, x] = value.astype(jnp.bfloat16)
    for d in range(1, R):
        gather_c(d).start()
    for e in range(1, X):
        gather_b(R, e).start()

    for f in range(frames):
        inv_rms, unit, normed, sigma = activate(f)
        grad_act = acc[f * height * width:(f + 1) * height * width]
        grad_normed = grad_act * sigma * (1.0 + normed * (1.0 - sigma))
        grad_unit = grad_normed * gain[...]
        along = jnp.sum(grad_unit * unit, axis=-1, keepdims=True) / channels
        result = inv_rms * (grad_unit - unit * along)
        gf_ref[f] = result.astype(jnp.bfloat16).reshape(height, width, channels)

    for d in range(1, R):
        gather_c(d).wait_recv()
        for e in range(1, X):
            gather_b(d, e).start()
    for d in (R, *range(1, R)):
        for e in range(1, X):
            gather_b(d, e).wait_recv()
        if PR == 2:
            gather_a(d).start()
    for d in (R, *range(1, R)):
        if PR == 2:
            gather_a(d).wait_recv()

    result_copy = pltpu.make_async_copy(gath, out_ref, out_sem)
    result_copy.start()
    for n in range(5):
        @pl.when(halos[n][0])
        def _():
            halo(n).wait_send()
    for d in order:
        if PR == 2:
            stage_a(d).wait_send()
            gather_a(d).wait_send()
        for e in range(1, X):
            stage_b(d, e).wait_send()
            gather_b(d, e).wait_send()
        if d < R:
            stage_c(d).wait_send()
            gather_c(d).wait_send()
    result_copy.wait()


def unpack(outputs, row_tiles, scale, tiles, out):
    group, per_group = out.shape[0], tiles.shape[0] // row_tiles
    sources = [
        tiles[lt * row_tiles:(lt + 1) * row_tiles].astype(jnp.float32).reshape(row_tiles * SUB, LANES)
        for lt in range(per_group)
    ]
    for a in range(group):
        value = rearrange(sources, LANES, a * outputs, outputs)
        out[a] = value[:, :outputs] * scale


def on_device(features, norm_gain, conv_weight, out_grad):
    frames, height, width, channels = features.shape
    outputs = out_grad.shape[3]
    T, R = lax.axis_size("tm"), lax.axis_size("rows")
    PR = 2 if T % 2 == 0 else 1
    X = T // PR
    kernels = conv_weight.shape[:3]
    taps = math.prod(kernels)
    group = LANES // math.gcd(LANES, outputs)
    per_group = group * outputs // LANES
    row_tiles = channels // SUB
    groups = -(-taps // group)
    m = -(-(groups * per_group * row_tiles) // (T * R))
    count = frames * height * width
    bf16, f32 = jnp.bfloat16, jnp.float32
    vmem, dma = pltpu.VMEM, pltpu.SemaphoreType.DMA
    tile = (m, SUB, LANES)
    rest = max(R - 1, 1)
    sides = max(X - 1, 1)
    in_vmem = pl.BlockSpec(memory_space=pltpu.VMEM)
    grad_features, gathered = pl.pallas_call(
        functools.partial(kernel, (T, R, PR, X, m)),
        out_shape=(
            jax.ShapeDtypeStruct(features.shape, bf16),
            jax.ShapeDtypeStruct((PR, R, X) + tile, bf16),
        ),
        in_specs=[in_vmem] * 4,
        out_specs=(in_vmem, pl.BlockSpec(memory_space=pl.ANY)),
        scratch_shapes=[
            vmem((frames + 2, height + 2, width, outputs), bf16),
            vmem((frames + 2, height + 2, width, 3 * LANES), bf16),
            vmem((channels, taps * LANES), bf16),
            vmem((channels, count), bf16),
            vmem((count, channels), f32),
            vmem((taps, channels, LANES), f32),
            vmem((PR, R, X) + tile, f32),
            vmem((PR, R, X) + tile, bf16),
            vmem((R, X) + tile, bf16),
            vmem((R, X) + tile, f32),
            vmem((R, X) + tile, bf16),
            vmem((R, sides) + tile, bf16),
            vmem(tile, f32),
            vmem((rest,) + tile, bf16),
            vmem((rest,) + tile, bf16),
            vmem((PR, R, X) + tile, bf16),
            dma((5,)), dma((5,)),
            dma((R,)), dma((R,)),
            dma((R, sides)), dma((R, sides)),
            dma((rest,)), dma((rest,)),
            dma((rest,)), dma((rest,)),
            dma((R, sides)), dma((R, sides)),
            dma((R,)), dma((R,)),
            dma(()),
        ],
        compiler_params=pltpu.CompilerParams(
            collective_id=0, has_side_effects=True, vmem_limit_bytes=50 * 1024 * 1024
        ),
    )(
        features, norm_gain.reshape(1, channels),
        conv_weight.reshape(taps, channels, outputs), out_grad,
    )
    scale = 1.0 / math.sqrt(count * T * R)
    grad_weight = pl.pallas_call(
        functools.partial(unpack, outputs, row_tiles, scale),
        grid=(groups,),
        in_specs=[pl.BlockSpec((per_group * row_tiles, SUB, LANES), lambda g: (g, 0, 0))],
        out_specs=pl.BlockSpec((group, channels, outputs), lambda g: (g, 0, 0)),
        out_shape=jax.ShapeDtypeStruct((taps, channels, outputs), f32),
    )(gathered.reshape(T * R * m, SUB, LANES))
    return grad_features, grad_weight.reshape(kernels + (channels, outputs))


def solution(mesh):
    split = P(("clips", "tm"), "rows", None, None)
    return jax.shard_map(
        on_device,
        mesh=mesh,
        in_specs=(split, P(), P(), split),
        out_specs=(split, P("clips", None, None, None, None)),
        check_vma=False,
    )
```

time: 163 us -> 47.6 us (0.29)
  waiting for transfers between devices: 96.8 us -> 0 us
  Pallas kernels: 0 us -> 40.9 us
  starting transfers between devices: 17.1 us -> 0 us
  matrix products: 16.7 us -> 0 us
  between operations: 14.7 us -> 0.66 us
  other arithmetic: 7.98 us -> 0 us
  local copies, waits for them, and re-layouts: 9.4 us -> 5.74 us
    psum x1 -> x0, waiting for transfers between devices: 96.7 us -> none  [on_device(): kernel_total = lax.psum(kernel_local, ('tm', 'rows'))]
    pallas_call x0 -> x2, Pallas kernels: none -> 40.9 us  [the longest x1 35.4 us: on_device(): pl.pallas_call(functools.partial(kernel, (T, R, PR, X, m)), out_shape=(ja...]
    ppermute x6 -> x0, starting transfers between devices: 17 us -> none  [the longest x2 10.1 us: with_halo(): lax.ppermute(tail, axis, [(i, (i + 1) % count) for i in range(ends)])]
    dot_general x54 -> x0, matrix products: 16.7 us -> none  [the longest x27 8.8 us: on_device(): jnp.dot(window.T, flat_out, preferred_element_type=jnp.float32)]
    reduce_sum x3 -> x0, other arithmetic: 2.98 us -> none  [the longest x2 1.59 us: activate(): jnp.mean(values * values, axis=-1, keepdims=True) + 1e-06]
    slice x5 -> x0, local copies, waits for them, and re-layouts: 2.8 us -> none  [the longest x1 0.95 us: on_device(): out_pad[2 - i:2 - i + frames, 2 - j:2 - j + height, 2 - k:2 - k + width]]
    convert_element_type x2 -> x0, other arithmetic: 2.1 us -> none  [the longest x1 1.45 us: on_device(): return (grad_features.astype(jnp.bfloat16), grad_weight)]
    mul x1 -> x0, other arithmetic: 1.71 us -> none  [on_device(): jnp.stack(kernel_terms).reshape(27 * channels, outputs) * scale]
  transfers between devices with their start and end apart: 7 -> 0, of which waited for: 1 -> 0; matrix products, arithmetic and copies ran while one was open for 10% -> 0% of each run, Pallas kernels for 0% -> 0%
where the time goes in v1:
time: 47.6 us; the launch traced here: 47.3 us
  Pallas kernels  40.9 us (86%)
  local copies, waits for them, and re-layouts  5.74 us (12%)
  between operations  0.66 us (1%)
    pallas_call x1, Pallas kernels, on_device(): pl.pallas_call(functools.partial(kernel, (T, R, PR, X, m)), out_shape=(ja...  35.4 us
    unnamed x11, local copies, waits for them, and re-layouts  5.74 us
    pallas_call x1, Pallas kernels, on_device(): pl.pallas_call(functools.partial(unpack, outputs, row_tiles, scale), grid...  5.45 us

profile of v1, /device:TPU:0, one launch (start us, length us, event | category | flops | bytes accessed | tf_op | source)
XLA Modules:
  0.0 47.3 jit_solution(5649426604061930241)
XLA Ops:
  0.6 0.0 copy-start
  0.6 1.3 %copy-done = bf16[3,3,3,192,96]{4,3,2,1,0:T(8,128)(2,1)S(1)} copy-done((bf16[3,3,3,192,96]{4,3,2,1,0:T(8,128)(2,1)S(1)}, bf16[3,3,3,192,96]{4,3,2,1,0:T(8,128)(2,1)}, u32[]{:S(2)}) %copy-start) | copy-done | bytes 995352
  2.0 0.0 copy-start.2
  2.0 1.0 %copy-done.2 = bf16[8,4,32,192]{3,2,1,0:T(8,128)(2,1)S(1)} copy-done((bf16[8,4,32,192]{3,2,1,0:T(8,128)(2,1)S(1)}, bf16[8,4,32,192]{3,2,1,0:T(8,128)(2,1)}, u32[]{:S(2)}) %copy-start.2) | copy-done | bytes 393240
  3.0 0.0 copy-start.3
  3.0 0.9 %copy-done.3 = bf16[8,4,32,96]{3,2,1,0:T(8,128)(2,1)S(1)} copy-done((bf16[8,4,32,96]{3,2,1,0:T(8,128)(2,1)S(1)}, bf16[8,4,32,96]{3,2,1,0:T(8,128)(2,1)}, u32[]{:S(2)}) %copy-start.3) | copy-done | bytes 196632
  3.9 0.0 copy-start.4
  3.9 0.7 %copy-done.4 = f32[192]{0:T(256)S(1)} copy-done((f32[192]{0:T(256)S(1)}, f32[192]{0:T(256)}, u32[]{:S(2)}) %copy-start.4) | copy-done | bytes 792
  4.6 35.4 %shard_map.59 = (bf16[8,4,32,192]{3,2,1,0:T(8,128)(2,1)S(1)}, bf16[2,4,2,16,16,128]{5,4,3,2,1,0:T(8,128)(2,1)S(1)}) custom-call(bf16[8,4,32,192]{3,2,1,0:T(8,128)(2,1)S(1)} %copy-done.2, f32[1,192]{1,0:T(1,128)S(1)} %bitcast.6, bf16[27,192,96]{2,1,0:T(8,128)(2,1)S(1)} %bitcast.4, bf16[8,4,32,96]{3,2,1,0:T(8,128)(2,1)S(1)} %copy-done.3), custom_call_target="tpu_custom_call" | custom-call | tf_op jit(solution)/shard_map/pallas_call | solution.py:324
  40.1 0.0 copy-start.1
  40.1 1.0 %copy-done.1 = bf16[2,4,2,16,16,128]{5,4,3,2,1,0:T(8,128)(2,1)} copy-done((bf16[2,4,2,16,16,128]{5,4,3,2,1,0:T(8,128)(2,1)}, bf16[2,4,2,16,16,128]{5,4,3,2,1,0:T(8,128)(2,1)S(1)}, u32[]{:S(2)}) %copy-start.1) | copy-done | bytes 1048600
  41.0 5.4 %shard_map.60 = f32[27,192,96]{2,1,0:T(8,128)} custom-call(bf16[256,16,128]{2,1,0:T(8,128)(2,1)} %bitcast.5), custom_call_target="tpu_custom_call" | custom-call | tf_op jit(solution)/shard_map/pallas_call | solution.py:366
  46.5 0.8 %copy.7 = bf16[8,4,32,192]{3,2,1,0:T(8,128)(2,1)} copy(bf16[8,4,32,192]{3,2,1,0:T(8,128)(2,1)S(1)} %get-tuple-element.8) | data formatting | bytes 786432
Async XLA Ops:
  0.6 1.3 %copy-start = (bf16[3,3,3,192,96]{4,3,2,1,0:T(8,128)(2,1)S(1)}, bf16[3,3,3,192,96]{4,3,2,1,0:T(8,128)(2,1)}, u32[]{:S(2)}) copy-start(bf16[3,3,3,192,96]{4,3,2,1,0:T(8,128)(2,1)} %param.6) | copy-start | bytes 2985988
  2.0 1.0 %copy-start.2 = (bf16[8,4,32,192]{3,2,1,0:T(8,128)(2,1)S(1)}, bf16[8,4,32,192]{3,2,1,0:T(8,128)(2,1)}, u32[]{:S(2)}) copy-start(bf16[8,4,32,192]{3,2,1,0:T(8,128)(2,1)} %features.1) | copy-start | bytes 1179652
  3.0 0.9 %copy-start.3 = (bf16[8,4,32,96]{3,2,1,0:T(8,128)(2,1)S(1)}, bf16[8,4,32,96]{3,2,1,0:T(8,128)(2,1)}, u32[]{:S(2)}) copy-start(bf16[8,4,32,96]{3,2,1,0:T(8,128)(2,1)} %grad.1) | copy-start | bytes 589828
  3.9 0.7 %copy-start.4 = (f32[192]{0:T(256)S(1)}, f32[192]{0:T(256)}, u32[]{:S(2)}) copy-start(f32[192]{0:T(256)} %param.5) | copy-start | bytes 2308
  40.1 1.0 %copy-start.1 = (bf16[2,4,2,16,16,128]{5,4,3,2,1,0:T(8,128)(2,1)}, bf16[2,4,2,16,16,128]{5,4,3,2,1,0:T(8,128)(2,1)S(1)}, u32[]{:S(2)}) copy-start(bf16[2,4,2,16,16,128]{5,4,3,2,1,0:T(8,128)(2,1)S(1)} %get-tuple-element.5) | copy-start | bytes 3145732

commit v2 on v1

v2 whole, which is shorter than its diff:
```python
import functools
import math

import jax
import jax.numpy as jnp
from jax import lax
from jax.experimental import pallas as pl
from jax.experimental.pallas import tpu as pltpu
from jax.sharding import PartitionSpec as P

LANES = 128
SUB = 16
MESH = pl.DeviceIdType.MESH
NT = (((1,), (1,)), ((), ()))


def shift_lanes(x, shift):
    shift = shift % LANES
    return x if shift == 0 else pltpu.roll(x, shift, 1)


def rearrange(sources, source_width, target_start, target_width):
    lane = lax.broadcasted_iota(jnp.int32, (1, LANES), 1)
    value = None
    for a, source in enumerate(sources):
        first = a * source_width - target_start
        if first >= target_width or first + source_width <= 0:
            continue
        moved = shift_lanes(source, first)
        value = moved if value is None else jnp.where(lane >= first, moved, value)
    return value


def kernel(
    dims,
    features_hbm, gain_hbm, weight_hbm, grad,
    gf_ref, out_ref,
    features, gain, weight, padded, shifted, wide, act_t, acc, parts, gwf, recv_a, sum_a,
    send_b, recv_b, sum_b, send_c, recv_c, gath,
    local, halo_s, halo_r, sa, ra, sb, rb, sc, rc, sc2, rc2, sb2, rb2, sa2, ra2,
):
    T, R, PR, X, U, m = dims
    frames, height, width, channels = features.shape
    outputs = grad.shape[3]
    taps = weight.shape[0]
    tm, z = lax.axis_index("tm"), lax.axis_index("rows")
    pair, x = lax.rem(tm, PR), lax.div(tm, PR)
    own = pl.ds(1, height)
    tail = pl.ds(frames, 2)
    body = pl.ds(0, frames)

    loads = [
        pltpu.make_async_copy(source, target, local.at[n])
        for n, (source, target) in enumerate((
            (features_hbm, features), (gain_hbm, gain),
            (grad, padded.at[body, own]), (weight_hbm, weight),
        ))
    ]
    for load in loads:
        load.start()

    barrier = pltpu.get_barrier_semaphore()
    for d in range(1, T * R):
        peer = lax.rem(tm * R + z + d, T * R)
        pl.semaphore_signal(
            barrier, inc=1, device_id={"tm": lax.div(peer, R), "rows": lax.rem(peer, R)},
            device_id_type=MESH,
        )

    up, down, later, earlier = z > 0, z < R - 1, tm < T - 1, tm > 0
    halos = (
        (down, (tm, z + 1), up, grad.at[:, height - 1], padded.at[body, 0]),
        (up, (tm, z - 1), down, grad.at[:, 0], padded.at[body, height + 1]),
        (earlier, (tm - 1, z), later, grad.at[pl.ds(0, 2)], padded.at[tail, own]),
        (jnp.logical_and(earlier, down), (tm - 1, z + 1), jnp.logical_and(later, up),
         grad.at[pl.ds(0, 2), height - 1], padded.at[tail, 0]),
        (jnp.logical_and(earlier, up), (tm - 1, z - 1), jnp.logical_and(later, down),
         grad.at[pl.ds(0, 2), 0], padded.at[tail, height + 1]),
    )

    def halo(n):
        _, to, _, source, target = halos[n]
        return pltpu.make_async_remote_copy(
            src_ref=source, dst_ref=target, send_sem=halo_s.at[n], recv_sem=halo_r.at[n],
            device_id={"tm": to[0], "rows": to[1]}, device_id_type=MESH,
        )

    for n, (_, _, receives, _, target) in enumerate(halos):
        @pl.when(jnp.logical_not(receives))
        def _():
            target[...] = jnp.zeros(target.shape, target.dtype)
    shifted[:, :, :, LANES:2 * LANES] = jnp.zeros(shifted.shape[:3] + (LANES,), shifted.dtype)

    pl.semaphore_wait(barrier, T * R - 1)
    for n in range(5):
        @pl.when(halos[n][0])
        def _():
            halo(n).start()

    def activate(f):
        values = features[f].reshape(height * width, channels).astype(jnp.float32)
        inv_rms = lax.rsqrt(jnp.sum(values * values, axis=-1, keepdims=True) / channels + 1e-06)
        unit = values * inv_rms
        normed = unit * gain[...]
        sigma = 1.0 / (1.0 + jnp.exp(-normed))
        return inv_rms, unit, normed, sigma

    loads[0].wait()
    loads[1].wait()
    for f in range(frames):
        _, _, normed, sigma = activate(f)
        act = (normed * sigma).astype(jnp.bfloat16)
        act_t[:, f * height * width:(f + 1) * height * width] = act.T

    loads[2].wait()
    for n in range(5):
        @pl.when(halos[n][2])
        def _():
            halo(n).wait_recv()

    rows = (height + 2) * width
    column = lax.rem(lax.broadcasted_iota(jnp.int32, (rows, LANES), 0), width)
    for f in range(frames + 2):
        shifted[f, :, :, LANES:LANES + outputs] = padded[f]
        middle = shifted[f, :, :, LANES:2 * LANES].reshape(rows, LANES).astype(jnp.float32)
        after = jnp.where(column == width - 1, 0.0, pltpu.roll(middle, rows - 1, 0))
        before = jnp.where(column == 0, 0.0, pltpu.roll(middle, 1, 0))
        shape = (height + 2, width, LANES)
        shifted[f, :, :, 0:LANES] = after.astype(jnp.bfloat16).reshape(shape)
        shifted[f, :, :, 2 * LANES:3 * LANES] = before.astype(jnp.bfloat16).reshape(shape)

    count = frames * height * width

    def window(i):
        return jnp.concatenate(
            [
                shifted[2 - i:2 - i + frames, 2 - j:2 - j + height].reshape(count, 3 * LANES)
                for j in range(3)
            ],
            axis=1,
        )

    def remote(source, target, send, recv, to_tm, to_z):
        return pltpu.make_async_remote_copy(
            src_ref=source, dst_ref=target, send_sem=send, recv_sem=recv,
            device_id={"tm": to_tm, "rows": to_z}, device_id_type=MESH,
        )

    mate = x * PR + (1 - pair if PR == 2 else pair)

    def chunk(d):
        return lax.rem(z + d, R)

    def back(d):
        return lax.rem(z + 2 * R - d, R)

    def side(e):
        return lax.rem(x + e, X)

    def stage_a(u, d):
        return remote(
            gwf.at[u, 1 - pair, chunk(d)], recv_a.at[u, d - 1],
            sa.at[u, d - 1], ra.at[u, d - 1], mate, z,
        )

    def stage_b(u, d, e):
        return remote(
            send_b.at[u, d - 1, side(e)], recv_b.at[u, d - 1, e - 1],
            sb.at[u, d - 1, e - 1], rb.at[u, d - 1, e - 1], side(e) * PR + pair, z,
        )

    def stage_c(u, d):
        return remote(
            send_c.at[u, d - 1], recv_c.at[u, d - 1],
            sc.at[u, d - 1], rc.at[u, d - 1], tm, chunk(d),
        )

    def gather_c(u, d):
        piece = gath.at[u, pair, z, x]
        return remote(piece, piece, sc2.at[u, d - 1], rc2.at[u, d - 1], tm, chunk(d))

    def gather_b(u, d, e):
        piece = gath.at[u, pair, back(d), x]
        return remote(
            piece, piece, sb2.at[u, d - 1, e - 1], rb2.at[u, d - 1, e - 1],
            side(e) * PR + pair, z,
        )

    def gather_a(u, d):
        piece = gath.at[u, pair, back(d)]
        return remote(piece, piece, sa2.at[u, d - 1], ra2.at[u, d - 1], mate, z)

    order = range(1, R + 1)
    mine_first = (R, *range(1, R))
    group = LANES // math.gcd(LANES, outputs)
    groups = -(-taps // group)
    per_group = group * outputs // LANES
    row_tiles = channels // SUB
    unit_tiles = T * R * m

    def place(n):
        n, s = divmod(n, m)
        n, xx = divmod(n, X)
        n, c = divmod(n, R)
        u, pp = divmod(n, PR)
        return u, pp, c, xx, s

    state = {"stored": 0, "sent": 0}

    def send_ready():
        while (state["sent"] + 1) * unit_tiles <= state["stored"]:
            if PR == 2:
                for d in order:
                    stage_a(state["sent"], d).start()
            state["sent"] += 1

    done = 0
    for i in range(3):
        terms = jnp.dot(act_t[...], window(i), preferred_element_type=jnp.float32)
        for t in range(9):
            parts[9 * i + t] = terms[:, t * LANES:(t + 1) * LANES]
        while done < groups and min(taps, (done + 1) * group) <= 9 * (i + 1):
            sources = [parts[t] for t in range(done * group, min(taps, (done + 1) * group))]
            for lt in range(per_group):
                tile = rearrange(sources, outputs, lt * LANES, LANES)
                for rt in range(row_tiles):
                    gwf[place(state["stored"])] = tile[rt * SUB:(rt + 1) * SUB]
                    state["stored"] += 1
            done += 1
        if i == 2:
            while state["stored"] < U * unit_tiles:
                gwf[place(state["stored"])] = jnp.zeros((SUB, LANES), jnp.float32)
                state["stored"] += 1
        send_ready()

    def conv(i):
        weights = wide[:, 9 * LANES * i:9 * LANES * (i + 1)]
        return lax.dot_general(window(i), weights, NT, preferred_element_type=jnp.float32)

    def after_a(u):
        for d in order:
            value = gwf[u, pair, chunk(d)]
            if PR == 2:
                stage_a(u, d).wait_recv()
                value = value + recv_a[u, d - 1]
            sum_a[u, d - 1] = value
            send_b[u, d - 1] = value.astype(jnp.bfloat16)
            for e in range(1, X):
                stage_b(u, d, e).start()

    def after_b(u):
        for d in order:
            value = sum_a[u, d - 1, x]
            for e in range(1, X):
                stage_b(u, d, e).wait_recv()
                value = value + recv_b[u, d - 1, e - 1].astype(jnp.float32)
            if d < R:
                send_c[u, d - 1] = value.astype(jnp.bfloat16)
                stage_c(u, d).start()
            else:
                sum_b[u] = value

    def after_c(u):
        value = sum_b[u]
        for d in range(1, R):
            stage_c(u, d).wait_recv()
            value = value + recv_c[u, d - 1].astype(jnp.float32)
        gath[u, pair, z, x] = value.astype(jnp.bfloat16)
        for d in range(1, R):
            gather_c(u, d).start()
        for e in range(1, X):
            gather_b(u, R, e).start()

    def after_gather_c(u):
        for d in range(1, R):
            gather_c(u, d).wait_recv()
            for e in range(1, X):
                gather_b(u, d, e).start()

    def after_gather_b(u):
        for d in mine_first:
            for e in range(1, X):
                gather_b(u, d, e).wait_recv()
            if PR == 2:
                gather_a(u, d).start()

    def after_gather_a(u):
        if PR == 2:
            for d in mine_first:
                gather_a(u, d).wait_recv()

    def unpack(g):
        first = g * per_group * row_tiles
        sources = [
            jnp.concatenate(
                [gath[place(first + lt * row_tiles + rt)] for rt in range(row_tiles)], axis=0
            ).astype(jnp.float32)
            for lt in range(per_group)
        ]
        for a in range(min(group, taps - g * group)):
            value = rearrange(sources, LANES, a * outputs, outputs)
            out_ref[g * group + a] = value[:, :outputs].astype(jnp.bfloat16)

    def finish_features(first, last):
        for f in range(first, last):
            inv_rms, unit, normed, sigma = activate(f)
            grad_act = acc[f * height * width:(f + 1) * height * width]
            grad_normed = grad_act * sigma * (1.0 + normed * (1.0 - sigma))
            grad_unit = grad_normed * gain[...]
            along = jnp.sum(grad_unit * unit, axis=-1, keepdims=True) / channels
            result = inv_rms * (grad_unit - unit * along)
            gf_ref[f] = result.astype(jnp.bfloat16).reshape(height, width, channels)

    after_a(0)
    loads[3].wait()
    wide[...] = jnp.zeros(wide.shape, wide.dtype)
    for t in range(taps):
        wide[:, t * LANES:t * LANES + outputs] = weight[t]
    for u in range(1, U):
        after_a(u)
    acc[...] = conv(0)
    after_b(0)
    acc[...] += conv(1)
    for u in range(1, U):
        after_b(u)
    after_c(0)
    acc[...] += conv(2)
    for u in range(1, U):
        after_c(u)
    after_gather_c(0)
    half = frames // 2
    finish_features(0, half)
    for u in range(1, U):
        after_gather_c(u)
    after_gather_b(0)
    finish_features(half, frames)
    for u in range(1, U):
        after_gather_b(u)
    unpacked = 0
    for u in range(U):
        after_gather_a(u)
        while unpacked < groups and (unpacked + 1) * per_group * row_tiles <= (u + 1) * unit_tiles:
            unpack(unpacked)
            unpacked += 1

    for n in range(5):
        @pl.when(halos[n][0])
        def _():
            halo(n).wait_send()
    for u in range(U):
        for d in order:
            if PR == 2:
                stage_a(u, d).wait_send()
                gather_a(u, d).wait_send()
            for e in range(1, X):
                stage_b(u, d, e).wait_send()
                gather_b(u, d, e).wait_send()
            if d < R:
                stage_c(u, d).wait_send()
                gather_c(u, d).wait_send()


def on_device(features, norm_gain, conv_weight, out_grad):
    frames, height, width, channels = features.shape
    outputs = out_grad.shape[3]
    T, R = lax.axis_size("tm"), lax.axis_size("rows")
    PR = 2 if T % 2 == 0 else 1
    X = T // PR
    U = 2
    kernels = conv_weight.shape[:3]
    taps = math.prod(kernels)
    group = LANES // math.gcd(LANES, outputs)
    per_group = group * outputs // LANES
    row_tiles = channels // SUB
    groups = -(-taps // group)
    m = -(-(groups * per_group * row_tiles) // (U * T * R))
    count = frames * height * width
    bf16, f32 = jnp.bfloat16, jnp.float32
    vmem, dma = pltpu.VMEM, pltpu.SemaphoreType.DMA
    tile = (m, SUB, LANES)
    rest = max(R - 1, 1)
    sides = max(X - 1, 1)
    in_vmem = pl.BlockSpec(memory_space=pltpu.VMEM)
    in_hbm = pl.BlockSpec(memory_space=pltpu.HBM)
    grad_features, kernel_sum = pl.pallas_call(
        functools.partial(kernel, (T, R, PR, X, U, m)),
        out_shape=(
            jax.ShapeDtypeStruct(features.shape, bf16),
            jax.ShapeDtypeStruct((taps, channels, outputs), bf16),
        ),
        in_specs=[in_hbm] * 4,
        out_specs=(in_vmem, in_vmem),
        scratch_shapes=[
            vmem(features.shape, bf16),
            vmem((1, channels), f32),
            vmem((taps, channels, outputs), bf16),
            vmem((frames + 2, height + 2, width, outputs), bf16),
            vmem((frames + 2, height + 2, width, 3 * LANES), bf16),
            vmem((channels, taps * LANES), bf16),
            vmem((channels, count), bf16),
            vmem((count, channels), f32),
            vmem((taps, channels, LANES), f32),
            vmem((U, PR, R, X) + tile, f32),
            vmem((U, R, X) + tile, f32),
            vmem((U, R, X) + tile, f32),
            vmem((U, R, X) + tile, bf16),
            vmem((U, R, sides) + tile, bf16),
            vmem((U,) + tile, f32),
            vmem((U, rest) + tile, bf16),
            vmem((U, rest) + tile, bf16),
            vmem((U, PR, R, X) + tile, bf16),
            dma((4,)),
            dma((5,)), dma((5,)),
            dma((U, R)), dma((U, R)),
            dma((U, R, sides)), dma((U, R, sides)),
            dma((U, rest)), dma((U, rest)),
            dma((U, rest)), dma((U, rest)),
            dma((U, R, sides)), dma((U, R, sides)),
            dma((U, R)), dma((U, R)),
        ],
        compiler_params=pltpu.CompilerParams(
            collective_id=0, has_side_effects=True, vmem_limit_bytes=50 * 1024 * 1024
        ),
    )(
        *(
            pltpu.with_memory_space_constraint(array, pltpu.HBM)
            for array in (
                features, norm_gain.reshape(1, channels),
                conv_weight.reshape(taps, channels, outputs), out_grad,
            )
        )
    )
    scale = 1.0 / math.sqrt(count * T * R)
    grad_weight = kernel_sum.astype(f32) * scale
    return grad_features, grad_weight.reshape(kernels + (channels, outputs))


def solution(mesh):
    split = P(("clips", "tm"), "rows", None, None)
    return jax.shard_map(
        on_device,
        mesh=mesh,
        in_specs=(split, P(), P(), split),
        out_specs=(split, P("clips", None, None, None, None)),
        check_vma=False,
    )
```

time: 47.6 us -> 38.6 us (0.81)
  Pallas kernels: 40.9 us -> 35 us
  local copies, waits for them, and re-layouts: 5.74 us -> 0.79 us
  other arithmetic: 0 us -> 1.81 us
    pallas_call x2 -> x1, Pallas kernels: 40.9 us -> 35 us  [on_device(): pl.pallas_call(functools.partial(kernel, (T, R, PR, X, U, m)), out_shape=...]
    unnamed x11 -> x1, local copies, waits for them, and re-layouts: 5.74 us -> 0.79 us
    mul x0 -> x1, other arithmetic: none -> 1.81 us  [on_device(): grad_weight = kernel_sum.astype(f32) * scale]
where the time goes in v2:
time: 38.6 us; the launch traced here: 38.2 us
  Pallas kernels  35 us (91%)
  other arithmetic  1.81 us (5%)
  local copies, waits for them, and re-layouts  0.79 us (2%)
  between operations  0.64 us (2%)
    pallas_call x1, Pallas kernels, on_device(): pl.pallas_call(functools.partial(kernel, (T, R, PR, X, U, m)), out_shape=...  35 us
    mul x1, other arithmetic, on_device(): grad_weight = kernel_sum.astype(f32) * scale  1.81 us
    unnamed x1, local copies, waits for them, and re-layouts  0.79 us

profile of v2, /device:TPU:0, one launch (start us, length us, event | category | flops | bytes accessed | tf_op | source)
XLA Modules:
  0.0 38.2 jit_solution(13825737696910056804)
XLA Ops:
  0.6 35.0 %shard_map.59 = (bf16[8,4,32,192]{3,2,1,0:T(8,128)(2,1)S(1)}, bf16[27,192,96]{2,1,0:T(8,128)(2,1)S(1)}) custom-call(bf16[8,4,32,192]{3,2,1,0:T(8,128)(2,1)} %features_hbm.1, f32[1,192]{1,0:T(1,128)} %bitcast.5, bf16[27,192,96]{2,1,0:T(8,128)(2,1)} %bitcast.4, bf16[8,4,32,96]{3,2,1,0:T(8,128)(2,1)} %grad.1), custom_call_target="tpu_custom_call" | custom-call | tf_op jit(solution)/shard_map/pallas_call | solution.py:385
  35.6 1.8 %convert_multiply_fusion = f32[27,192,96]{2,1,0:T(8,128)} fusion(bf16[27,192,96]{2,1,0:T(8,128)(2,1)S(1)} %get-tuple-element.5), kind=kLoop, calls=%fused_computation | loop fusion | flops 995328 | bytes 2985984 | tf_op jit(solution)/shard_map/mul | solution.py:434
  37.5 0.8 %copy.7 = bf16[8,4,32,192]{3,2,1,0:T(8,128)(2,1)} copy(bf16[8,4,32,192]{3,2,1,0:T(8,128)(2,1)S(1)} %get-tuple-element.8) | data formatting | bytes 786432

commit v3 on v2

--- a/solution.py
+++ b/solution.py
@@ -191,7 +191,9 @@
         return remote(piece, piece, sa2.at[u, d - 1], ra2.at[u, d - 1], mate, z)
 
     order = range(1, R + 1)
-    mine_first = (R, *range(1, R))
+    low = 1 - lax.div(2 * z, R)
+    nearest = [low * (R - d) + (1 - low) * d for d in range(1, R)]
+    mine_first = (R, *nearest)
     group = LANES // math.gcd(LANES, outputs)
     groups = -(-taps // group)
     per_group = group * outputs // LANES
@@ -272,7 +274,7 @@
             gather_b(u, R, e).start()
 
     def after_gather_c(u):
-        for d in range(1, R):
+        for d in nearest:
             gather_c(u, d).wait_recv()
             for e in range(1, X):
                 gather_b(u, d, e).start()

time: 38.6 us -> 37.9 us (0.982)
  Pallas kernels: 35 us -> 34.3 us
    pallas_call x1, Pallas kernels: 35 us -> 34.3 us  [on_device(): pl.pallas_call(functools.partial(kernel, (T, R, PR, X, U, m)), out_shape=...]
where the time goes in v3:
time: 37.9 us; the launch traced here: 37.6 us
  Pallas kernels  34.3 us (91%)
  other arithmetic  1.81 us (5%)
  local copies, waits for them, and re-layouts  0.79 us (2%)
  between operations  0.64 us (2%)
    pallas_call x1, Pallas kernels, on_device(): pl.pallas_call(functools.partial(kernel, (T, R, PR, X, U, m)), out_shape=...  34.3 us
    mul x1, other arithmetic, on_device(): grad_weight = kernel_sum.astype(f32) * scale  1.81 us
    unnamed x1, local copies, waits for them, and re-layouts  0.79 us

profile of v3, /device:TPU:0, one launch (start us, length us, event | category | flops | bytes accessed | tf_op | source)
XLA Modules:
  0.0 37.6 jit_solution(428285711705549809)
XLA Ops:
  0.6 34.3 %shard_map.59 = (bf16[8,4,32,192]{3,2,1,0:T(8,128)(2,1)S(1)}, bf16[27,192,96]{2,1,0:T(8,128)(2,1)S(1)}) custom-call(bf16[8,4,32,192]{3,2,1,0:T(8,128)(2,1)} %features_hbm.1, f32[1,192]{1,0:T(1,128)} %bitcast.5, bf16[27,192,96]{2,1,0:T(8,128)(2,1)} %bitcast.4, bf16[8,4,32,96]{3,2,1,0:T(8,128)(2,1)} %grad.1), custom_call_target="tpu_custom_call" | custom-call | tf_op jit(solution)/shard_map/pallas_call | solution.py:387
  35.0 1.8 %convert_multiply_fusion = f32[27,192,96]{2,1,0:T(8,128)} fusion(bf16[27,192,96]{2,1,0:T(8,128)(2,1)S(1)} %get-tuple-element.5), kind=kLoop, calls=%fused_computation | loop fusion | flops 995328 | bytes 2985984 | tf_op jit(solution)/shard_map/mul | solution.py:436
  36.8 0.8 %copy.7 = bf16[8,4,32,192]{3,2,1,0:T(8,128)(2,1)} copy(bf16[8,4,32,192]{3,2,1,0:T(8,128)(2,1)S(1)} %get-tuple-element.8) | data formatting | bytes 786432
